TPU v7x, 512 devices: a whole 4x8x8 slice. The times are simulated.
512 devices in a mesh: samp: 32 (over x, y_lo, core), var: 16 (over z, y_hi).
Axes of the slice: x: 4, y: 8 (y_hi: 2, y_lo: 4; y = y_hi * 4 + y_lo), z: 8, core: 2. Of those that a mesh axis runs over, the one named last changes fastest.
Arguments:
- genotypes: bfloat16 [16384, 40960], P('samp', 'var'), may hold values from 0 to 2, as said below
- imputed: bfloat16 [16384, 20480], P('samp', 'var'), may hold values from 0 to 2, as said below
- centre: int32 [16384], P('samp'), may hold values from 0 to 21, as said below
- phenotypes: float32 [8, 16384], P(None, 'samp'), may hold values from -6 to 6
- earlier: float32 [8, 16384], P(None, 'samp'), may hold values from -6 to 6
- genetic: float32 [8], replicated, may hold values from 0.2 to 2
- noise: float32 [8], replicated, may hold values from 0.2 to 2
Outputs:
- solution: float32 [8, 16384], P(None, ('samp', 'var'))
- residual: float32 [8, 16384], P(None, ('samp', 'var'))
- scores: float32 [8, 20480], P(None, 'var')
Inputs may be any that keep to these rules, and one draw needn't show every extreme that they name: `genotypes`: allele dosages 0, 1 or 2; every variant has its own allele frequency. `imputed`: allele dosages 0, 1 or 2; every variant has its own allele frequency. One of 22 centres; a centre may have no samples.
All inputs are finite; a program needn't handle non-finite values.
Results may differ from a plain program's by a relative error of at most 0.033.
Values may be sent and summed in bfloat16 or wider, within the bound.
No kernel may reach another device: no remote copies, remote signals or barrier semaphores. Data moves between devices by JAX's collectives and lax.ppermute only.
A program may use at most 64 MiB of HBM per device.

v0:
```python
import jax
import jax.numpy as jnp
from jax import lax
from jax.sharding import PartitionSpec as P

M = 40960
CENTRES = 22
ITERS = 2


def inner(values):
    return lax.psum((values[0],), "samp")


def operate(direction, standard, genetic, noise):
    low = direction.astype(jnp.bfloat16)
    partial_proj = jnp.dot(low, standard, preferred_element_type=jnp.float32)
    scale_row = (genetic / M)[:, None]
    summed_proj = lax.psum(partial_proj, "samp")
    scaled = (summed_proj * scale_row).astype(jnp.bfloat16)
    partial_back = lax.dot_general(
        scaled, standard, (((1,), (1,)), ((), ())), preferred_element_type=jnp.float32
    )
    back = lax.psum(partial_back, "var")
    return back + noise[:, None] * direction


def shards(genotypes, imputed, centre, phenotypes, earlier, genetic, noise):
    rows = genotypes.shape[0]
    total = rows * lax.axis_size("samp")
    share = rows // lax.axis_size("var")
    offset = lax.axis_index("var") * share
    values = genotypes.astype(jnp.float32)
    dosage = imputed.astype(jnp.float32)
    onehot = (centre[:, None] == jnp.arange(CENTRES, dtype=jnp.int32)[None, :]).astype(jnp.float32)
    sums = lax.psum(
        (
            jnp.sum(values, axis=0),
            jnp.sum(values * values, axis=0),
            jnp.sum(dosage, axis=0),
            jnp.sum(dosage * dosage, axis=0),
            jnp.dot(earlier, dosage, precision=lax.Precision.HIGHEST),
            jnp.dot(phenotypes, onehot, precision=lax.Precision.HIGHEST),
            jnp.sum(onehot, axis=0),
            jnp.sum(earlier, axis=1),
            jnp.sum(earlier * earlier, axis=1),
        ),
        "samp",
    )
    gen_sum, gen_sq, imp_sum, imp_sq, imp_cross, centre_sum, counts, earlier_sum, earlier_sq = sums
    mean_col = gen_sum / total
    var_col = gen_sq / total - mean_col * mean_col
    standard = ((values - mean_col[None, :]) * lax.rsqrt(var_col + 1e-05)[None, :]).astype(
        jnp.bfloat16
    )
    imp_mean = imp_sum / total
    imp_var = imp_sq / total - imp_mean * imp_mean + 1e-05
    earlier_var = earlier_sq / total + 1e-05
    cross = imp_cross - earlier_sum[:, None] * imp_mean[None, :]
    scores = cross / jnp.sqrt(total * imp_var[None, :] * earlier_var[:, None])
    centre_mean = centre_sum / jnp.maximum(counts, 1.0)[None, :]
    centred = phenotypes - jnp.dot(centre_mean, onehot.T, precision=lax.Precision.HIGHEST)
    solution = jnp.zeros_like(centred)
    residual = centred
    direction = residual
    (norm_now,) = inner((jnp.sum(residual * residual, axis=1),))
    for step in range(ITERS):
        image = operate(direction, standard, genetic, noise)
        (curve,) = inner((jnp.sum(direction * image, axis=1),))
        alpha = norm_now / curve
        solution = solution + alpha[:, None] * direction
        residual = residual - alpha[:, None] * image
        if step + 1 < ITERS:
            (norm_next,) = inner((jnp.sum(residual * residual, axis=1),))
            direction = residual + (norm_next / norm_now)[:, None] * direction
            norm_now = norm_next
    solution = lax.dynamic_slice_in_dim(solution, offset, share, 1)
    residual = lax.dynamic_slice_in_dim(residual, offset, share, 1)
    return (solution, residual, scores)


def solution(mesh):
    in_specs = (
        P("samp", "var"),
        P("samp", "var"),
        P("samp"),
        P(None, "samp"),
        P(None, "samp"),
        P(),
        P(),
    )
    out_specs = (P(None, ("samp", "var")), P(None, ("samp", "var")), P(None, "var"))
    return jax.shard_map(shards, mesh=mesh, in_specs=in_specs, out_specs=out_specs, check_vma=False)
```

profile of v0, /device:TPU:64, one launch (start us, length us, event | category | flops | bytes accessed | tf_op | source)
XLA Modules:
  0.0 1123.9 jit_solution(7656716114734789581)
XLA Ops:
  7.2 2.5 convert_reduce_fusion
  9.8 0.1 convert_reduce_fusion.2
  9.9 0.1 convolution_bitcast_fusion
  10.1 138.6 %all-reduce.2 = (f32[8,22]{0,1:T(8,128)S(1)}, f32[22]{0:T(128)S(1)}, f32[2560]{0:T(1024)S(1)}, f32[2560]{0:T(1024)S(1)}) all-reduce(f32[8,22]{0,1:T(8,128)S(1)} %convolution_bitcast_fusion, f32[22]{0:T(128)S(1)} %convert_reduce_fusion.2, f32[2560]{0:T(1024)S(1)} %get-tuple-element.4, ...), channel_id=1, replica_groups=mesh['samp'=32,'var'=16] {'samp'}, use_global_device_ids=true, to_apply=%region_0.0 | all-reduce | flops 5318 | bytes 42544 | tf_op jit(solution)/shard_map/psum | solution.py:36
  148.7 0.3 convolution_subtract_fusion
  149.0 3.1 fusion.10
  152.2 0.6 fusion.22
  152.8 0.4 convert_reduce_fusion.1
  153.2 248.6 %all-reduce.6.cloned.1.call-done = f32[8,2560]{1,0:T(8,128)} async-done(((f32[8,2560]{1,0:T(8,128)}), f32[8,2560]{1,0:T(8,128)}) %all-reduce.6.cloned.1.call-update) | async-done | bytes 81936 | tf_op jit(solution)/shard_map/psum | solution.py:19
  401.7 2.6 fusion.8
  404.3 97.8 %psum.125 = f32[8,512]{1,0:T(8,128)S(1)} all-reduce(f32[8,512]{1,0:T(8,128)S(1)} %fusion.8), channel_id=1, replica_groups=mesh['samp'=32,'var'=16] {'var'}, use_global_device_ids=true, to_apply=%region_10.0 | all-reduce | flops 4096 | bytes 32768 | tf_op jit(solution)/shard_map/psum | solution.py:24
  502.2 0.2 multiply_reduce_fusion.3
  502.3 67.4 %all-reduce.1 = (f32[8]{0:T(128)S(1)}, f32[8]{0:T(128)S(1)}) all-reduce(f32[8]{0:T(128)S(1)} %get-tuple-element.10, f32[8]{0:T(128)S(1)} %get-tuple-element.9), channel_id=1, replica_groups=mesh['samp'=32,'var'=16] {'samp'}, use_global_device_ids=true, to_apply=%region_4.0 | all-reduce | flops 16 | bytes 128 | tf_op jit(solution)/shard_map/psum | solution.py:12
  569.7 0.2 multiply_reduce_fusion.2
  569.9 67.4 %psum.127 = f32[8]{0:T(128)S(1)} all-reduce(f32[8]{0:T(128)S(1)} %get-tuple-element.25), channel_id=1, replica_groups=mesh['samp'=32,'var'=16] {'samp'}, use_global_device_ids=true, to_apply=%region_14.0 | all-reduce | flops 8 | bytes 64 | tf_op jit(solution)/shard_map/psum | solution.py:12
  637.4 1.3 fusion.6
  638.7 0.1 fusion.21
  638.9 243.8 %all-reduce.8.cloned.1.call-done = f32[8,2560]{1,0:T(8,128)} async-done(((f32[8,2560]{1,0:T(8,128)}), f32[8,2560]{1,0:T(8,128)}) %all-reduce.8.cloned.1.call-update) | async-done | bytes 81936 | tf_op jit(solution)/shard_map/psum | solution.py:19
  882.6 1.7 fusion.4
  884.3 97.8 %psum.129 = f32[8,512]{1,0:T(8,128)S(1)} all-reduce(f32[8,512]{1,0:T(8,128)S(1)} %fusion.4), channel_id=1, replica_groups=mesh['samp'=32,'var'=16] {'var'}, use_global_device_ids=true, to_apply=%region_16.0 | all-reduce | flops 4096 | bytes 32768 | tf_op jit(solution)/shard_map/psum | solution.py:24
  982.2 0.2 multiply_reduce_fusion.1
  982.3 133.3 %all-reduce = (f32[8]{0:T(128)S(1)}, f32[8,1280]{1,0:T(8,128)S(1)}, f32[8]{0:T(128)S(1)}, f32[1280]{0:T(1024)S(1)}, f32[1280]{0:T(1024)S(1)}, /*index=5*/f32[8]{0:T(128)S(1)}) all-reduce(f32[8]{0:T(128)S(1)} %get-tuple-element.23, f32[8,1280]{1,0:T(8,128)S(1)} %fusion.22, ...), channel_id=1, replica_groups=mesh['samp'=32,'var'=16] {'samp'}, use_global_device_ids=true, to_apply=%region_18.0 | all-reduce | flops 12824 | bytes 102592 | tf_op jit(solution)/shard_map/psum | solution.py:12
  1115.7 0.7 dynamic-slice_subtract_fusion
  1116.3 0.7 rsqrt_multiply_fusion
  (27 shorter events, 0.3 us)
Async XLA Ops:
  7.2 2.6 copy-start.4
  7.2 2.7 copy-start.3
  7.2 394.6 %all-reduce.6.cloned.1.call-start = ((), (), s32[]{:S(2)}) async-start(), calls=%async_computation | async-start | bytes 163840 | tf_op jit(solution)/shard_map/psum | solution.py:19
  9.8 142.3 %copy-start.6 = (f32[8]{0:T(128)S(1)}, f32[8]{0:T(128)}, u32[]{:S(2)}) copy-start(f32[8]{0:T(128)} %param.12) | copy-start | bytes 100
  9.8 142.4 %copy-start = (bf16[512,1280]{1,0:T(8,128)(2,1)S(1)}, bf16[512,1280]{1,0:T(8,128)(2,1)}, u32[]{:S(2)}) copy-start(bf16[512,1280]{1,0:T(8,128)(2,1)} %param.8) | copy-start | bytes 3932164
  9.8 142.4 %copy-start.2 = (f32[8,512]{1,0:T(8,128)S(1)}, f32[8,512]{1,0:T(8,128)}, u32[]{:S(2)}) copy-start(f32[8,512]{1,0:T(8,128)} %param.11) | copy-start | bytes 49156
  152.1 730.6 %all-reduce.8.cloned.1.call-start = ((), (), s32[]{:S(2)}) async-start(), calls=%async_computation.1 | async-start | bytes 163840 | tf_op jit(solution)/shard_map/psum | solution.py:19
  152.8 349.4 %copy-start.5 = (f32[8]{0:T(128)S(1)}, f32[8]{0:T(128)}, u32[]{:S(2)}) copy-start(f32[8]{0:T(128)} %param.13) | copy-start | bytes 100
  153.2 484.2 %copy-start.1 = (bf16[512,2560]{1,0:T(8,128)(2,1)S(1)}, bf16[512,2560]{1,0:T(8,128)(2,1)}, u32[]{:S(2)}) copy-start(bf16[512,2560]{1,0:T(8,128)(2,1)} %param.7) | copy-start | bytes 7864324
Sparse Core Ops, SparseCore 0:
  152.2 249.5 all-reduce.5
  638.8 243.7 all-reduce.7
where the time goes:
time: 1120 us
  blocking collectives  602 us (54%)
  waiting for transfers between devices  492 us (44%)
  between operations  14.2 us (1%)
    psum x2, waiting for transfers between devices, operate(): summed_proj = lax.psum(partial_proj, 'samp')  492 us
    psum x3, blocking collectives, inner(): return lax.psum((values[0],), 'samp')  268 us
    psum x2, blocking collectives, operate(): back = lax.psum(partial_back, 'var')  196 us
    psum x1, blocking collectives, shards(): lax.psum((jnp.sum(values, axis=0), jnp.sum(values * values, axis=0), jnp....  139 us
  transfers between devices with their start and end apart: 2, of which 2 were waited for; matrix products, arithmetic and copies ran while one was open for 0% of the time, Pallas kernels for 0%

commit v1 on v0

--- a/solution.py
+++ b/solution.py
@@ -8,6 +8,11 @@
 ITERS = 2
 
 
+def add_all(value, mesh_axis):
+    parts = lax.all_gather(value, mesh_axis)
+    return jnp.sum(parts, axis=0)
+
+
 def inner(values):
     return lax.psum((values[0],), "samp")
 
@@ -16,7 +21,7 @@
     low = direction.astype(jnp.bfloat16)
     partial_proj = jnp.dot(low, standard, preferred_element_type=jnp.float32)
     scale_row = (genetic / M)[:, None]
-    summed_proj = lax.psum(partial_proj, "samp")
+    summed_proj = add_all(partial_proj, "samp")
     scaled = (summed_proj * scale_row).astype(jnp.bfloat16)
     partial_back = lax.dot_general(
         scaled, standard, (((1,), (1,)), ((), ())), preferred_element_type=jnp.float32

time: 1120 us -> 750 us (0.67)
  waiting for transfers between devices: 492 us -> 118 us
    psum x2 -> x0, waiting for transfers between devices: 492 us -> none  [operate(): summed_proj = lax.psum(partial_proj, 'samp')]
    all_gather x0 -> x2, waiting for transfers between devices: none -> 118 us  [add_all(): parts = lax.all_gather(value, mesh_axis)]
where the time goes in v1:
time: 750 us
  blocking collectives  600 us (80%)
  waiting for transfers between devices  118 us (16%)
  between operations  14.2 us (2%)
  other arithmetic  9.13 us (1%)
  matrix products  8.76 us (1%)
    psum x3, blocking collectives, inner(): return lax.psum((values[0],), 'samp')  268 us
    psum x2, blocking collectives, operate(): back = lax.psum(partial_back, 'var')  193 us
    psum x1, blocking collectives, shards(): lax.psum((jnp.sum(values, axis=0), jnp.sum(values * values, axis=0), jnp....  138 us
    all_gather x2, waiting for transfers between devices, add_all(): parts = lax.all_gather(value, mesh_axis)  118 us
  transfers between devices with their start and end apart: 2, of which 2 were waited for; matrix products, arithmetic and copies ran while one was open for 0% of the time, Pallas kernels for 0%

profile of v1, /device:TPU:64, one launch (start us, length us, event | category | flops | bytes accessed | tf_op | source)
XLA Modules:
  0.0 750.1 jit_solution(793936042653474028)
XLA Ops:
  7.2 2.7 convert_reduce_fusion
  10.2 138.5 %all-reduce.2 = (f32[8,22]{0,1:T(8,128)S(1)}, f32[22]{0:T(128)S(1)}, f32[2560]{0:T(1024)S(1)}, f32[2560]{0:T(1024)S(1)}) all-reduce(f32[8,22]{0,1:T(8,128)S(1)} %convolution_bitcast_fusion, f32[22]{0:T(128)S(1)} %convert_reduce_fusion.2, f32[2560]{0:T(1024)S(1)} %get-tuple-element.4, ...), channel_id=1, replica_groups=mesh['samp'=32,'var'=16] {'samp'}, use_global_device_ids=true, to_apply=%region_0.0 | all-reduce | flops 5318 | bytes 42544 | tf_op jit(solution)/shard_map/psum | solution.py:41
  148.7 0.3 convolution_subtract_fusion
  149.0 1.3 fusion.10
  150.4 62.3 %all-gather.5.cloned.1.call-done = f32[256,2560]{1,0:T(8,128)} async-done(((f32[8,2560]{1,0:T(8,128)}), f32[256,2560]{1,0:T(8,128)}) %all-gather.5.cloned.1.call-update) | async-done | bytes 2621456 | tf_op jit(solution)/shard_map/all_gather | solution.py:12
  212.8 1.9 bitcast_reduce_fusion.1
  214.6 0.8 fusion.8
  215.4 96.8 %psum.110 = f32[8,512]{1,0:T(8,128)S(1)} all-reduce(f32[8,512]{1,0:T(8,128)S(1)} %fusion.8), channel_id=1, replica_groups=mesh['samp'=32,'var'=16] {'var'}, use_global_device_ids=true, to_apply=%region_10.0 | all-reduce | flops 4096 | bytes 32768 | tf_op jit(solution)/shard_map/psum | solution.py:29
  312.2 0.2 multiply_reduce_fusion.3
  312.4 67.5 %all-reduce.1 = (f32[8]{0:T(128)S(1)}, f32[8]{0:T(128)S(1)}) all-reduce(f32[8]{0:T(128)S(1)} %get-tuple-element.10, f32[8]{0:T(128)S(1)} %get-tuple-element.9), channel_id=1, replica_groups=mesh['samp'=32,'var'=16] {'samp'}, use_global_device_ids=true, to_apply=%region_4.0 | all-reduce | flops 16 | bytes 128 | tf_op jit(solution)/shard_map/psum | solution.py:17
  379.9 0.2 multiply_reduce_fusion.2
  380.1 67.4 %psum.112 = f32[8]{0:T(128)S(1)} all-reduce(f32[8]{0:T(128)S(1)} %get-tuple-element.25), channel_id=1, replica_groups=mesh['samp'=32,'var'=16] {'samp'}, use_global_device_ids=true, to_apply=%region_14.0 | all-reduce | flops 8 | bytes 64 | tf_op jit(solution)/shard_map/psum | solution.py:17
  447.5 3.1 fusion.6
  450.7 0.1 fusion.21
  450.8 0.4 convert_reduce_fusion.1
  451.2 0.6 fusion.22
  451.8 55.5 %all-gather.7.cloned.1.call-done = f32[256,2560]{1,0:T(8,128)} async-done(((f32[8,2560]{1,0:T(8,128)}), f32[256,2560]{1,0:T(8,128)}) %all-gather.7.cloned.1.call-update) | async-done | bytes 2621456 | tf_op jit(solution)/shard_map/all_gather | solution.py:12
  507.3 1.9 bitcast_reduce_fusion
  509.2 2.5 fusion.4
  511.7 96.7 %psum.113 = f32[8,512]{1,0:T(8,128)S(1)} all-reduce(f32[8,512]{1,0:T(8,128)S(1)} %fusion.4), channel_id=1, replica_groups=mesh['samp'=32,'var'=16] {'var'}, use_global_device_ids=true, to_apply=%region_16.0 | all-reduce | flops 4096 | bytes 32768 | tf_op jit(solution)/shard_map/psum | solution.py:29
  608.4 0.2 multiply_reduce_fusion.1
  608.5 133.3 %all-reduce = (f32[8]{0:T(128)S(1)}, f32[8,1280]{1,0:T(8,128)S(1)}, f32[8]{0:T(128)S(1)}, f32[1280]{0:T(1024)S(1)}, f32[1280]{0:T(1024)S(1)}, /*index=5*/f32[8]{0:T(128)S(1)}) all-reduce(f32[8]{0:T(128)S(1)} %get-tuple-element.23, f32[8,1280]{1,0:T(8,128)S(1)} %fusion.22, ...), channel_id=1, replica_groups=mesh['samp'=32,'var'=16] {'samp'}, use_global_device_ids=true, to_apply=%region_18.0 | all-reduce | flops 12824 | bytes 102592 | tf_op jit(solution)/shard_map/psum | solution.py:17
  741.9 0.7 dynamic-slice_subtract_fusion
  742.5 0.7 rsqrt_multiply_fusion
  (29 shorter events, 0.5 us)
Async XLA Ops:
  7.2 141.8 %copy-start.1 = (bf16[512,2560]{1,0:T(8,128)(2,1)S(1)}, bf16[512,2560]{1,0:T(8,128)(2,1)}, u32[]{:S(2)}) copy-start(bf16[512,2560]{1,0:T(8,128)(2,1)} %param.7) | copy-start | bytes 7864324
  7.2 2.7 copy-start.4
  7.2 2.9 copy-start.3
  7.2 205.6 %all-gather.5.cloned.1.call-start = ((), (), s32[]{:S(2)}) async-start(), calls=%async_computation | async-start | bytes 2703360 | tf_op jit(solution)/shard_map/all_gather | solution.py:12
  9.9 140.5 %copy-start.6 = (f32[8]{0:T(128)S(1)}, f32[8]{0:T(128)}, u32[]{:S(2)}) copy-start(f32[8]{0:T(128)} %param.12) | copy-start | bytes 100
  150.3 356.9 %all-gather.7.cloned.1.call-start = ((), (), s32[]{:S(2)}) async-start(), calls=%async_computation.1 | async-start | bytes 2703360 | tf_op jit(solution)/shard_map/all_gather | solution.py:12
  150.4 161.8 %copy-start.5 = (f32[8]{0:T(128)S(1)}, f32[8]{0:T(128)}, u32[]{:S(2)}) copy-start(f32[8]{0:T(128)} %param.13) | copy-start | bytes 100
  215.4 235.2 %copy-start.2 = (f32[8,512]{1,0:T(8,128)S(1)}, f32[8,512]{1,0:T(8,128)}, u32[]{:S(2)}) copy-start(f32[8,512]{1,0:T(8,128)} %param.11) | copy-start | bytes 49156
  215.4 235.4 %copy-start = (bf16[512,1280]{1,0:T(8,128)(2,1)S(1)}, bf16[512,1280]{1,0:T(8,128)(2,1)}, u32[]{:S(2)}) copy-start(bf16[512,1280]{1,0:T(8,128)(2,1)} %param.8) | copy-start | bytes 3932164
Sparse Core Ops, SparseCore 0:
  150.5 62.2 all-gather.4
  450.8 56.4 all-gather.6
